TPU v7x, 256 devices: a whole 4x4x8 slice. The times are simulated.
256 devices in a mesh: seq: 64 (over x, z_hi, y), dp: 4 (over z_lo, core).
Axes of the slice: x: 4, y: 4, z: 8 (z_hi: 4, z_lo: 2; z = z_hi * 2 + z_lo), core: 2. Of those that a mesh axis runs over, the one named last changes fastest.
Arguments:
- tokens: bfloat16 [32768, 1024], P(('dp', 'seq')), parts along dimension 0, may hold values from -6 to 6
- norm_gain: float32 [1024], replicated, may hold values from 0.1 to 1.9
- filters: float32 [12, 8192], P(None, 'seq'), may hold values from -0.0625 to 0.0625
- mixing: bfloat16 [12, 1024, 1024], P(None, 'seq'), may hold values from -0.0546875 to 0.0546875
Outputs:
- mixed: bfloat16 [32768, 1024], P(('dp', 'seq')), parts along dimension 0
There are 4 independent parts, one for each index of `dp`. A program takes and returns all parts, laid end to end along the dimension named above; an argument that names none is the same for every part. Nothing has to cross between parts.
All inputs are finite; a program needn't handle non-finite values.
Results may differ from a plain program's by a relative error of at most 0.0044.
Values may be sent and summed in bfloat16 or wider, within the bound.
A program may use at most 192 MiB of HBM per device.

v0:
```python
import math

import jax
import jax.numpy as jnp
from jax import lax
from jax.sharding import PartitionSpec as P

radix = 128
highest = lax.Precision.HIGHEST


def cos_sin(rows, cols, total):
    left = lax.broadcasted_iota(jnp.int32, (rows, cols), 0)
    right = lax.broadcasted_iota(jnp.int32, (rows, cols), 1)
    angle = (left * right % total).astype(jnp.float32) * (2.0 * math.pi / total)
    return (jnp.cos(angle), jnp.sin(angle))


def make_tables(blocks):
    total = blocks * radix
    half = blocks // 2
    cos_outer, sin_outer = cos_sin(blocks, half, blocks)
    cos_twid, sin_twid = cos_sin(blocks, radix, total)
    cos_inner, sin_inner = cos_sin(radix, radix, radix)
    cos_back, sin_back = cos_sin(half, blocks, blocks)
    return (
        cos_outer,
        sin_outer,
        cos_twid,
        sin_twid,
        cos_inner,
        sin_inner,
        cos_back,
        sin_back,
        total,
    )


def forward(signal, tables):
    cos_outer, sin_outer, cos_twid, sin_twid, cos_inner, sin_inner, cos_back, sin_back, total = (
        tables
    )
    first_re = jnp.einsum("kn,cna->cka", cos_outer, signal, precision=highest)
    first_im = -jnp.einsum("kn,cna->cka", sin_outer, signal, precision=highest)
    twist_re = first_re * cos_twid + first_im * sin_twid
    twist_im = first_im * cos_twid - first_re * sin_twid
    out_re = jnp.einsum("cka,aj->ckj", twist_re, cos_inner, precision=highest) + jnp.einsum(
        "cka,aj->ckj", twist_im, sin_inner, precision=highest
    )
    out_im = jnp.einsum("cka,aj->ckj", twist_im, cos_inner, precision=highest) - jnp.einsum(
        "cka,aj->ckj", twist_re, sin_inner, precision=highest
    )
    return (out_re, out_im)


def inverse(spec_re, spec_im, tables):
    cos_outer, sin_outer, cos_twid, sin_twid, cos_inner, sin_inner, cos_back, sin_back, total = (
        tables
    )
    inner_re = jnp.einsum("ckj,aj->cka", spec_re, cos_inner, precision=highest) - jnp.einsum(
        "ckj,aj->cka", spec_im, sin_inner, precision=highest
    )
    inner_im = jnp.einsum("ckj,aj->cka", spec_im, cos_inner, precision=highest) + jnp.einsum(
        "ckj,aj->cka", spec_re, sin_inner, precision=highest
    )
    twist_re = inner_re * cos_twid - inner_im * sin_twid
    twist_im = inner_im * cos_twid + inner_re * sin_twid
    result = jnp.einsum("nk,cka->cna", cos_back, twist_re, precision=highest) - jnp.einsum(
        "nk,cka->cna", sin_back, twist_im, precision=highest
    )
    return result / total


def local(tokens, norm_gain, filters, mixing):
    tok_rows, width = tokens.shape
    groups = lax.axis_size("seq")
    values = tokens.astype(jnp.float32)
    scale_row = lax.rsqrt(jnp.mean(values * values, axis=1, keepdims=True) + 1e-05)
    normed = (values * scale_row * norm_gain).astype(jnp.bfloat16)
    taps = lax.all_gather(filters, "seq", axis=1, tiled=True)
    num_filters, length = taps.shape
    blocks = 2 * length // radix
    half = blocks // 2
    tables = make_tables(blocks)
    phi_re, phi_im = forward(taps.reshape(num_filters, half, radix), tables)
    grouped = normed.reshape(tok_rows, groups, width // groups)
    piece = lax.all_to_all(grouped, "seq", split_axis=1, concat_axis=0, tiled=True)
    count = piece.shape[2]
    signal = piece[:, 0, :].astype(jnp.float32).T.reshape(count, half, radix)
    sig_re, sig_im = forward(signal, tables)

    def per_filter(spectrum):
        filt_re, filt_im = spectrum
        prod_re = sig_re * filt_re - sig_im * filt_im
        prod_im = sig_re * filt_im + sig_im * filt_re
        return inverse(prod_re, prod_im, tables).reshape(count, length).astype(jnp.bfloat16)

    features = lax.map(per_filter, (phi_re, phi_im))
    back = lax.all_to_all(features, "seq", split_axis=2, concat_axis=1, tiled=True)
    branch = jnp.einsum(
        "kct,kcd->td",
        back,
        lax.all_gather(mixing, "seq", axis=1, tiled=True),
        preferred_element_type=jnp.float32,
    )
    return (values + branch).astype(jnp.bfloat16)


def solution(mesh):
    in_specs = (P(("dp", "seq"), None), P(), P(None, "seq"), P(None, "seq", None))
    out_specs = P(("dp", "seq"), None)
    return jax.shard_map(local, mesh=mesh, in_specs=in_specs, out_specs=out_specs, check_vma=False)
```

profile of v0, /device:TPU:32, one launch (start us, length us, event | category | flops | bytes accessed | tf_op | source)
XLA Modules:
  0.0 559.1 jit_solution(12533361922189063383)
XLA Ops:
  10.3 13.7 %all-to-all-start = ((bf16[128,64,16]{0,2,1:T(8,128)(2,1)}), bf16[128,64,16]{0,2,1:T(8,128)(2,1)S(1)}, u32[]{:S(2)}, u32[]{:S(2)}) async-start(bf16[128,64,16]{0,2,1:T(8,128)(2,1)} %bitcast.6), calls=%async_computation | async-start | bytes 524288 | tf_op jit(solution)/shard_map/all_to_all | solution.py:87
  24.4 222.2 %all_gather.6 = f32[12,8192]{1,0:T(8,128)S(1)} all-gather(f32[12,128]{1,0:T(8,128)} %param.8), channel_id=1, replica_groups=mesh['seq'=64,'dp'=4] {'seq'}, dimensions={1}, use_global_device_ids=true | all-gather | bytes 399360 | tf_op jit(solution)/shard_map/all_gather | solution.py:80
  251.8 1.9 convolution_add_fusion.2
  255.5 2.0 fusion.102
  257.5 2.2 fusion.103
  259.7 2.0 convolution_add_fusion.1
  261.7 2.0 convolution_subtract_fusion.2
  263.7 106.2 %while.12 = (s32[]{:T(128)}, bf16[12,16,8192]{2,1,0:T(8,128)(2,1)}, f32[12,128,128]{2,1,0:T(8,128)}, f32[16,128,128]{2,1,0:T(8,128)S(1)}, f32[12,128,128]{2,1,0:...) while((s32[]{:T(128)}, bf16[12,16,8192]{2,1,0:T(8,128)(2,1)}, ...), condition=%wide.region_2.3_spmd.clone.clone, body=%wide.region_1.2_spmd.clone.clone.sunk | while | flops 2020278272 | bytes 22413904 | solution.py:98
  264.6 1.2 fusion.225
  282.3 1.2 fusion.225
  293.6 1.2 fusion.224
  320.2 1.2 fusion.224
  326.5 1.2 fusion.225
  329.0 1.2 fusion.224
  344.2 1.2 fusion.225
  353.1 1.2 fusion.225
  355.6 1.2 fusion.224
  361.9 1.2 fusion.225
  369.9 27.1 %copy.39 = bf16[12,16,8192]{1,0,2:T(8,128)(2,1)} copy(bf16[12,16,8192]{2,1,0:T(8,128)(2,1)} %get-tuple-element.79) | data formatting | bytes 6291456 | tf_op jit(solution)/shard_map/while | solution.py:98
  397.0 34.7 %reshape.71 = bf16[64,2,12288]{2,1,0:T(2,128)(2,1)S(1)} reshape(bf16[8192,12,16]{2,1,0:T(8,128)(2,1)} %bitcast.116) | data formatting | bytes 6291456
  431.7 46.9 %all_to_all.33 = bf16[64,2,12288]{2,1,0:T(2,128)(2,1)} all-to-all(bf16[64,2,12288]{2,1,0:T(2,128)(2,1)S(1)} %reshape.71), channel_id=1, replica_groups=mesh['seq'=64,'dp'=4] {'seq'}, dimensions={0} | all-to-all | bytes 6291456 | tf_op jit(solution)/shard_map/all_to_all | solution.py:99
  478.6 34.0 %reshape.72 = bf16[8192,12,16]{2,1,0:T(8,128)(2,1)} reshape(bf16[64,2,12288]{2,1,0:T(2,128)(2,1)} %all_to_all.33) | data formatting | bytes 6291456
  512.6 28.9 %copy.41 = bf16[12,64,16,128]{3,2,1,0:T(8,128)(2,1)S(1)} copy(bf16[12,64,16,128]{2,0,3,1:T(8,128)(2,1)} %bitcast.117) | data formatting | bytes 6291456 | tf_op jit(solution)/shard_map/all_to_all | solution.py:99
  541.5 10.7 %fusion.89 = bf16[128,1024]{1,0:T(8,128)(2,1)} fusion(bf16[12,1024,128]{2,1,0:T(8,128)(2,1)S(1)} %bitcast.118, bf16[12,1024,1024]{2,1,0:T(8,128)(2,1)} %all-gather.2.cloned.1.call-done, bf16[128,1024]{1,0:T(8,128)(2,1)S(1)} %copy-done), kind=kOutput, calls=%fused_computation.102 | convolution fusion | flops 3221618688 | bytes 28835840 | tf_op jit(solution)/shard_map/kct,kcd->td/dot_general | solution.py:100
  (135 shorter events, 104.1 us)
Async XLA Ops:
  6.5 535.0 %all-gather.2.cloned.1.call-start = ((), (), s32[]{:S(2)}) async-start(), calls=%async_computation.2 | async-start | bytes 25559040 | tf_op jit(solution)/shard_map/all_gather | solution.py:103
  10.3 243.4 %all-to-all-start = ((bf16[128,64,16]{0,2,1:T(8,128)(2,1)}), bf16[128,64,16]{0,2,1:T(8,128)(2,1)S(1)}, u32[]{:S(2)}, u32[]{:S(2)}) async-start(bf16[128,64,16]{0,2,1:T(8,128)(2,1)} %bitcast.6), calls=%async_computation | async-start | bytes 524288 | tf_op jit(solution)/shard_map/all_to_all | solution.py:87
  512.6 28.9 %copy-start = (bf16[128,1024]{1,0:T(8,128)(2,1)S(1)}, bf16[128,1024]{1,0:T(8,128)(2,1)}, u32[]{:S(2)}) copy-start(bf16[128,1024]{1,0:T(8,128)(2,1)} %param.6) | copy-start | bytes 786436
Sparse Core Ops, SparseCore 0:
  10.7 238.2 all-gather.1
where the time goes:
time: 563 us; the launch traced here: 559 us
  blocking collectives  269 us (48%)
  local copies, waits for them, and re-layouts  146 us (26%)
  matrix products  109 us (19%)
  starting transfers between devices  13.7 us (2%)
  between operations  13.6 us (2%)
  other arithmetic  5.77 us (1%)
    all_gather x1, blocking collectives, local(): taps = lax.all_gather(filters, 'seq', axis=1, tiled=True)  222 us
    unnamed x7, local copies, waits for them, and re-layouts  69 us
    all_to_all x1, blocking collectives, local(): lax.all_to_all(features, 'seq', split_axis=2, concat_axis=1, tiled=True)  46.9 us
    all_to_all x1, local copies, waits for them, and re-layouts, local(): lax.all_to_all(features, 'seq', split_axis=2, concat_axis=1, tiled=True)  28.9 us
    while x1, local copies, waits for them, and re-layouts, local(): features = lax.map(per_filter, (phi_re, phi_im))  27.1 us
    dot_general x12, matrix products, inverse(): jnp.einsum('ckj,aj->cka', spec_im, cos_inner, precision=highest)  14.9 us
    dot_general x12, matrix products, inverse(): jnp.einsum('ckj,aj->cka', spec_re, cos_inner, precision=highest)  14.9 us
    dot_general x12, matrix products, inverse(): jnp.einsum('ckj,aj->cka', spec_im, sin_inner, precision=highest)  14.8 us
  transfers between devices with their start and end apart: 2, of which 0 were waited for; matrix products, arithmetic and copies ran while one was open for 45% of the time, Pallas kernels for 0%

commit v1 on v0

v1 whole, which is shorter than its diff:
```python
import jax
import jax.numpy as jnp
from jax import lax
from jax.experimental import pallas as pl
from jax.experimental.pallas import tpu as pltpu
from jax.sharding import Mesh, PartitionSpec as P

AXES = ("x", "zh", "y", "zl", "q")
BLK = 128
NB = 64
GRP = 256
HALF = 6
PAD = 3


def remote(src, dst, send, recv, **where):
    return pltpu.make_async_remote_copy(
        src_ref=src,
        dst_ref=dst,
        send_sem=send,
        recv_sem=recv,
        device_id=where,
        device_id_type=pl.DeviceIdType.MESH,
    )


def kernel(
    tok_ref, gain_ref, filt_ref, mix_ref, out_ref,
    normed, taps, shifted, rolled, sig, acc, feats, weights, part_send, part_recv, part_own,
    red_send, red_recv, home_tok, fin,
    f_send, f_recv, n_send, n_recv, n_loc, t_send, t_recv, y_send, y_recv, z_send, z_recv,
    p_send, p_recv, wz_send, wz_recv, wy_send, wy_recv, w_loc, q_send, q_recv, x_send, x_recv,
    h_send, h_recv,
):
    x = lax.axis_index("x")
    zh = lax.axis_index("zh")
    y = lax.axis_index("y")
    zl = lax.axis_index("zl")
    q = lax.axis_index("q")
    me = (x * 4 + zh) * 4 + y
    to = {"zh": 2 * zl + q, "zl": zh % 2, "q": zh // 2}
    src = {"zh": 2 * q + zl, "zl": zh // 2, "q": zh % 2}
    own = jnp.logical_and(zh == 2 * zl + q, jnp.logical_and(zl == zh % 2, q == zh // 2))
    other = jnp.logical_not(own)
    idx_own = 8 * q + 4 * zl + y

    barrier = pltpu.get_barrier_semaphore()

    def greet(**where):
        pl.semaphore_signal(barrier, inc=1, device_id=where, device_id_type=pl.DeviceIdType.MESH)

    def greet_seq(d, carry):
        @pl.when(d != me)
        def _():
            greet(x=d // 16, zh=(d // 4) % 4, y=d % 4)

        return carry

    greet(q=1 - q)
    greet(zl=1 - zl)
    lax.fori_loop(0, NB, greet_seq, 0)
    for d in range(4):
        there = (x + d) % 4
        if d == 0:

            @pl.when(other)
            def _():
                greet(x=there, **to)
                greet(x=there, **src)
        else:
            greet(x=there, **to)
            greet(x=there, **src)

    values = tok_ref[...].astype(jnp.float32)
    scale_row = lax.rsqrt(jnp.mean(values * values, axis=1, keepdims=True) + 1e-05)
    normed[...] = (values * scale_row * gain_ref[...]).astype(jnp.bfloat16)
    taps[me] = filt_ref[q]

    pl.semaphore_wait(barrier, jnp.where(own, 71, 73).astype(jnp.int32))

    def first(d):
        to_x = (x + d) % 4
        return remote(
            normed.at[:, pl.ds(pl.multiple_of(GRP * to_x, GRP), GRP)],
            sig.at[x, 4 * zh + y],
            n_send.at[d],
            n_recv.at[d],
            x=to_x,
            **to,
        )

    def first_arrival(d):
        from_x = (x + 4 - d) % 4
        return remote(
            sig.at[from_x, idx_own], sig.at[from_x, idx_own], n_send.at[d], n_recv.at[d], x=from_x, **src
        )

    local_first = pltpu.make_async_copy(
        normed.at[:, pl.ds(pl.multiple_of(GRP * x, GRP), GRP)], sig.at[x, idx_own], n_loc.at[0]
    )
    tok_copy = remote(tok_ref, home_tok, t_send.at[0], t_recv.at[0], x=x, **to)
    local_tok = pltpu.make_async_copy(tok_ref, home_tok, n_loc.at[1])

    for d in range(1, 4):
        first(d).start()

    @pl.when(other)
    def _():
        first(0).start()

    @pl.when(own)
    def _():
        local_first.start()

    def tap_copy(d):
        return remote(
            filt_ref.at[q], taps.at[me], f_send.at[d], f_recv.at[me], x=d // 16, zh=(d // 4) % 4, y=d % 4
        )

    def tap_arrival(d):
        return remote(taps.at[d], taps.at[d], f_send.at[d], f_recv.at[d], x=d // 16, zh=(d // 4) % 4, y=d % 4)

    def send_taps(d, carry):
        @pl.when(d != me)
        def _():
            tap_copy(d).start()

        return carry

    lax.fori_loop(0, NB, send_taps, 0)

    mine = mix_ref.at[pl.ds(HALF * q, HALF)]

    def wz(e):
        return remote(mine, weights.at[:, 4 * zh + y], wz_send.at[e - 1], wz_recv.at[e - 1], zh=(zh + e) % 4)

    def wz_arrival(e):
        there = weights.at[:, 4 * ((zh + 4 - e) % 4) + y]
        return remote(there, there, wz_send.at[e - 1], wz_recv.at[e - 1], zh=(zh + e) % 4)

    def wy(e, d):
        held = weights.at[:, 4 * ((zh + 4 - e) % 4) + y]
        return remote(held, held, wy_send.at[e, d - 1], wy_recv.at[e, d - 1], y=(y + d) % 4)

    def wy_arrival(e, d):
        there = weights.at[:, 4 * ((zh + 4 - e) % 4) + (y + 4 - d) % 4]
        return remote(there, there, wy_send.at[e, d - 1], wy_recv.at[e, d - 1], y=(y + d) % 4)

    local_mix = pltpu.make_async_copy(mine, weights.at[:, 4 * zh + y], w_loc.at[0])
    local_mix.start()
    for e in range(1, 4):
        wz(e).start()

    @pl.when(other)
    def _():
        tok_copy.start()

    @pl.when(own)
    def _():
        local_tok.start()

    def shard(zl_src, d):
        return sig.at[:, 8 * q + 4 * zl_src + (y + 4 - d) % 4]

    def ycopy(d):
        return remote(shard(zl, 0), shard(zl, 0), y_send.at[d - 1], y_recv.at[d - 1], y=(y + d) % 4)

    def y_arrival(d):
        return remote(shard(zl, d), shard(zl, d), y_send.at[d - 1], y_recv.at[d - 1], y=(y + d) % 4)

    def zcopy(d):
        return remote(shard(zl, d), shard(zl, d), z_send.at[d], z_recv.at[d], zl=1 - zl)

    def z_arrival(d):
        return remote(shard(1 - zl, d), shard(1 - zl, d), z_send.at[d], z_recv.at[d], zl=1 - zl)

    def pcopy(far, d):
        held = shard(1 - zl if far else zl, d)
        return remote(held, held, p_send.at[4 * far + d], p_recv.at[4 * far + d], q=1 - q)

    def p_arrival(far, d):
        there = sig.at[:, 8 * (1 - q) + 4 * (1 - zl if far else zl) + (y + 4 - d) % 4]
        return remote(there, there, p_send.at[4 * far + d], p_recv.at[4 * far + d], q=1 - q)

    for d in range(1, 4):
        first_arrival(d).wait_recv()

    @pl.when(other)
    def _():
        first_arrival(0).wait_recv()

    @pl.when(own)
    def _():
        local_first.wait()

    for d in range(1, 4):
        ycopy(d).start()
    zcopy(0).start()
    pcopy(0, 0).start()

    def wait_taps(d, carry):
        @pl.when(d != me)
        def _():
            tap_arrival(d).wait_recv()

        return carry

    lax.fori_loop(0, NB, wait_taps, 0)

    rolled[...] = jnp.zeros_like(rolled)
    shifted[:, NB * BLK :] = jnp.zeros((HALF * BLK, PAD * BLK), jnp.bfloat16)
    causal = lax.broadcasted_iota(jnp.int32, (BLK, BLK), 1) <= lax.broadcasted_iota(jnp.int32, (BLK, BLK), 0)

    def build(m, carry):
        lanes = pl.ds(pl.multiple_of(BLK * (NB - 1 - m), BLK), BLK)
        for k in range(HALF):
            rows = slice(BLK * k, BLK * (k + 1))
            line = jnp.broadcast_to(taps[m, k : k + 1, :], (BLK, BLK))
            now = pltpu.roll(line, 1, 1, stride=1, stride_axis=0)
            shifted[rows, lanes] = jnp.where(causal, now, rolled[rows, :]).astype(jnp.bfloat16)
            rolled[rows, :] = now
        return carry

    lax.fori_loop(0, NB, build, 0)

    for d in range(1, 4):
        y_arrival(d).wait_recv()
        zcopy(d).start()
        pcopy(0, d).start()
    local_mix.wait()
    for d in range(1, 4):
        wy(0, d).start()
    for d in range(4):
        z_arrival(d).wait_recv()
        pcopy(1, d).start()
    for e in range(1, 4):
        wz_arrival(e).wait_recv()
        for d in range(1, 4):
            wy(e, d).start()
    for d in range(4):
        p_arrival(0, d).wait_recv()
        p_arrival(1, d).wait_recv()

    def conv(slot):
        which = jnp.where(slot < 4, 1 - q, q)
        i = 16 * (slot % 4) + 8 * which + 4 * zl + y
        first_lane = BLK * (NB - 1 - i)
        acc[...] = jnp.zeros_like(acc)

        def chunk(c, carry):
            lhs = shifted[:, pl.ds(pl.multiple_of(first_lane + 4 * BLK * c, BLK), 4 * BLK)]
            rhs = sig[c // 4, pl.ds(4 * (c % 4), 4)].reshape(4 * BLK, GRP)
            acc[...] += jnp.dot(lhs, rhs, preferred_element_type=jnp.float32)
            return carry

        lax.fori_loop(0, (i + 4) // 4, chunk, 0)
        for k in range(HALF):
            feats[pl.ds(pl.multiple_of(BLK * slot, BLK), BLK), GRP * k : GRP * (k + 1)] = acc[
                BLK * k : BLK * (k + 1), :
            ].astype(jnp.bfloat16)

    def project(base, n):
        rows = feats[base : base + 4 * BLK, :]
        cols = pl.ds(pl.multiple_of(256 * n, 256), 256)
        return cols, jnp.dot(
            rows, weights[:, :, :, cols].reshape(HALF * GRP, 256), preferred_element_type=jnp.float32
        )

    def conv_step(slot, carry):
        conv(slot)
        return carry

    lax.fori_loop(0, 4, conv_step, 0)

    for e in range(4):
        for d in range(1, 4):
            wy_arrival(e, d).wait_recv()

    def project_send(n, carry):
        cols, value = project(0, n)
        part_send[:, cols] = value.astype(jnp.bfloat16)
        return carry

    lax.fori_loop(0, 4, project_send, 0)
    swap = remote(part_send, part_recv, q_send.at[0], q_recv.at[0], q=1 - q)
    swap.start()

    lax.fori_loop(4, 8, conv_step, 0)

    swap.wait_recv()

    def project_own(n, carry):
        cols, value = project(4 * BLK, n)
        total = value + part_recv[:, cols].astype(jnp.float32)
        part_own[:, cols] = total
        red_send[:, cols] = total.astype(jnp.bfloat16)
        return carry

    lax.fori_loop(0, 4, project_own, 0)

    def red(d):
        there = (x + d) % 4
        return remote(
            red_send.at[pl.ds(pl.multiple_of(BLK * there, BLK), BLK)],
            red_recv.at[d - 1],
            x_send.at[d - 1],
            x_recv.at[d - 1],
            x=there,
        )

    for d in range(1, 4):
        red(d).start()

    @pl.when(other)
    def _():
        tok_copy.wait_recv()

    @pl.when(own)
    def _():
        local_tok.wait()

    for d in range(1, 4):
        red(d).wait_recv()
    total = part_own[pl.ds(pl.multiple_of(BLK * x, BLK), BLK), :]
    for d in range(1, 4):
        total = total + red_recv[d - 1].astype(jnp.float32)
    fin[...] = (home_tok[...].astype(jnp.float32) + total).astype(jnp.bfloat16)

    back = remote(fin, out_ref, h_send.at[0], h_recv.at[0], x=x, **src)
    local_back = pltpu.make_async_copy(fin, out_ref, n_loc.at[2])

    @pl.when(other)
    def _():
        back.start()

    @pl.when(own)
    def _():
        local_back.start()
        local_back.wait()

    for d in range(1, 4):
        first(d).wait_send()
        ycopy(d).wait_send()
        wz(d).wait_send()
        red(d).wait_send()
        for e in range(4):
            wy(e, d).wait_send()
    for d in range(4):
        zcopy(d).wait_send()
        pcopy(0, d).wait_send()
        pcopy(1, d).wait_send()
    swap.wait_send()

    def wait_sent(d, carry):
        @pl.when(d != me)
        def _():
            tap_copy(d).wait_send()

        return carry

    lax.fori_loop(0, NB, wait_sent, 0)

    @pl.when(other)
    def _():
        first(0).wait_send()
        tok_copy.wait_send()
        back.wait_send()
        back.wait_recv()


def local(tokens, norm_gain, filters, mixing):
    rows, width = tokens.shape
    count = filters.shape[0]
    flipped = jnp.flip(filters, axis=1).reshape(2, count // 2, BLK)
    flipped = jnp.pad(flipped, ((0, 0), (0, 8 - count // 2), (0, 0)))
    bf16, f32 = jnp.bfloat16, jnp.float32
    dma = pltpu.SemaphoreType.DMA
    vmem = pl.BlockSpec(memory_space=pltpu.VMEM)
    return pl.pallas_call(
        kernel,
        out_shape=jax.ShapeDtypeStruct((rows, width), bf16),
        in_specs=[vmem] * 4,
        out_specs=vmem,
        scratch_shapes=[
            pltpu.VMEM((rows, width), bf16),
            pltpu.VMEM((NB, 8, BLK), f32),
            pltpu.VMEM((HALF * BLK, (NB + PAD) * BLK), bf16),
            pltpu.VMEM((HALF * BLK, BLK), f32),
            pltpu.VMEM((4, 16, BLK, GRP), bf16),
            pltpu.VMEM((HALF * BLK, GRP), f32),
            pltpu.VMEM((8 * BLK, HALF * GRP), bf16),
            pltpu.VMEM((HALF, 16, 16, width), bf16),
            pltpu.VMEM((4 * BLK, width), bf16),
            pltpu.VMEM((4 * BLK, width), bf16),
            pltpu.VMEM((4 * BLK, width), f32),
            pltpu.VMEM((4 * BLK, width), bf16),
            pltpu.VMEM((3, BLK, width), bf16),
            pltpu.VMEM((rows, width), bf16),
            pltpu.VMEM((rows, width), bf16),
            dma((NB,)), dma((NB,)), dma((4,)), dma((4,)), dma((3,)), dma((1,)), dma((1,)),
            dma((3,)), dma((3,)), dma((4,)), dma((4,)), dma((8,)), dma((8,)),
            dma((3,)), dma((3,)), dma((4, 3)), dma((4, 3)), dma((1,)), dma((1,)), dma((1,)),
            dma((3,)), dma((3,)), dma((1,)), dma((1,)),
        ],
        compiler_params=pltpu.CompilerParams(
            collective_id=0, has_side_effects=True, vmem_limit_bytes=56 * 1024 * 1024
        ),
    )(tokens, norm_gain.reshape(1, width), flipped, mixing)


def solution(mesh):
    grid = Mesh(mesh.devices.reshape(4, 4, 4, 2, 2), AXES)
    seq = ("x", "zh", "y")
    in_specs = (P(("zl", "q") + seq, None), P(), P(None, seq), P(None, seq, None))
    out_specs = P(("zl", "q") + seq, None)
    return jax.shard_map(local, mesh=grid, in_specs=in_specs, out_specs=out_specs, check_vma=False)
```

time: 563 us -> 140 us (0.25)
  blocking collectives: 269 us -> 0 us
  local copies, waits for them, and re-layouts: 146 us -> 3.05 us
  Pallas kernels: 0 us -> 137 us
  matrix products: 109 us -> 0 us
  starting transfers between devices: 13.7 us -> 0 us
  between operations: 13.6 us -> 0.01 us
  other arithmetic: 5.77 us -> 0 us
    all_gather x1 -> x0, blocking collectives: 222 us -> none  [local(): taps = lax.all_gather(filters, 'seq', axis=1, tiled=True)]
    pallas_call x0 -> x1, Pallas kernels: none -> 137 us  [local(): pl.pallas_call(kernel, out_shape=jax.ShapeDtypeStruct((rows, width), bf16...]
    dot_general x85 -> x0, matrix products: 109 us -> none  [the longest x12 14.9 us: inverse(): jnp.einsum('ckj,aj->cka', spec_im, cos_inner, precision=highest)]
    unnamed x7 -> x1, local copies, waits for them, and re-layouts: 69 us -> 1.67 us
    all_to_all x1 -> x0, blocking collectives: 46.9 us -> none  [local(): lax.all_to_all(features, 'seq', split_axis=2, concat_axis=1, tiled=True)]
    all_to_all x2 -> x0, local copies, waits for them, and re-layouts: 29 us -> none  [the longest x1 28.9 us: local(): lax.all_to_all(features, 'seq', split_axis=2, concat_axis=1, tiled=True)]
    while x1 -> x0, local copies, waits for them, and re-layouts: 27.1 us -> none  [local(): features = lax.map(per_filter, (phi_re, phi_im))]
    all_to_all x1 -> x0, starting transfers between devices: 13.7 us -> none  [local(): lax.all_to_all(grouped, 'seq', split_axis=1, concat_axis=0, tiled=True)]
  transfers between devices with their start and end apart: 2 -> 0, of which waited for: 0 -> 0; matrix products, arithmetic and copies ran while one was open for 45% -> 0% of each run, Pallas kernels for 0% -> 0%
where the time goes in v1:
time: 140 us
  Pallas kernels  137 us (98%)
  local copies, waits for them, and re-layouts  3.05 us (2%)
    pallas_call x1, Pallas kernels, local(): pl.pallas_call(kernel, out_shape=jax.ShapeDtypeStruct((rows, width), bf16...  137 us

profile of v1, /device:TPU:32, one launch (start us, length us, event | category | flops | bytes accessed | tf_op | source)
XLA Modules:
  0.0 140.0 jit_solution(15096827586550125509)
XLA Ops:
  0.0 0.8 rev.4
  0.8 0.6 pad.4.filt_ref
  1.4 136.9 %shard_map.46 = bf16[128,1024]{1,0:T(8,128)(2,1)} custom-call(bf16[128,1024]{1,0:T(8,128)(2,1)} %tok_ref.1, f32[1,1024]{1,0:T(1,128)} %bitcast.1, f32[2,8,128]{2,1,0:T(8,128)} %pad.4.filt_ref, bf16[12,16,1024]{2,1,0:T(8,128)(2,1)} %mix_ref.1), custom_call_target="tpu_custom_call" | custom-call | tf_op jit(solution)/shard_map/pallas_call | solution.py:379
  138.3 1.7 %copy.6 = bf16[128,1024]{1,0:T(8,128)(2,1)} copy(bf16[128,1024]{1,0:T(8,128)(2,1)} %shard_map.46) | data formatting | bytes 524288
  (1 shorter events, 0.0 us)

commit v2 on v1

v2 whole, which is shorter than its diff:
```python
import jax
import jax.numpy as jnp
from jax import lax
from jax.experimental import pallas as pl
from jax.experimental.pallas import tpu as pltpu
from jax.sharding import Mesh, PartitionSpec as P

AXES = ("x", "zh", "y", "zl", "q")
BLK = 128
NB = 64
GRP = 256
HALF = 6
PAD = 3
PIECE = 32
AROUND = [(a, b, c) for a in range(4) for b in range(4) for c in range(4) if a + b + c > 0]
ROWS = 384


def remote(src, dst, send, recv, **where):
    return pltpu.make_async_remote_copy(
        src_ref=src,
        dst_ref=dst,
        send_sem=send,
        recv_sem=recv,
        device_id=where,
        device_id_type=pl.DeviceIdType.MESH,
    )


def kernel(
    tok_ref, gain_ref, filt_ref, mix_ref, out_ref,
    normed, tap_own, taps, shifted, rolled, sig, acc, feats, weights, part_send, part_recv, part_own,
    red_send, red_recv, home_tok, fin,
    f_send, f_recv, n_send, n_recv, n_loc, t_send, t_recv, y_send, y_recv, z_send, z_recv,
    p_send, p_recv, wz_send, wz_recv, wy_send, wy_recv, w_loc, q_send, q_recv, x_send, x_recv,
    h_send, h_recv, h_loc,
):
    x = lax.axis_index("x")
    zh = lax.axis_index("zh")
    y = lax.axis_index("y")
    zl = lax.axis_index("zl")
    q = lax.axis_index("q")
    me = (x * 4 + zh) * 4 + y
    to = {"zh": 2 * zl + q, "zl": zh % 2, "q": zh // 2}
    src = {"zh": 2 * q + zl, "zl": zh // 2, "q": zh % 2}
    own = jnp.logical_and(zh == 2 * zl + q, jnp.logical_and(zl == zh % 2, q == zh // 2))
    other = jnp.logical_not(own)
    idx_own = 8 * q + 4 * zl + y
    xs = [(x + d) % 4 for d in range(4)]
    zhs = [(zh + d) % 4 for d in range(4)]
    ys = [(y + d) % 4 for d in range(4)]

    barrier = pltpu.get_barrier_semaphore()

    def greet(**where):
        pl.semaphore_signal(barrier, inc=1, device_id=where, device_id_type=pl.DeviceIdType.MESH)

    greet(q=1 - q)
    greet(zl=1 - zl)
    for dx, dz, dy in AROUND:
        greet(x=xs[dx], zh=zhs[dz], y=ys[dy])
    for d in range(4):
        there = (x + d) % 4
        if d == 0:

            @pl.when(other)
            def _():
                greet(x=there, **to)
                greet(x=there, **src)
        else:
            greet(x=there, **to)
            greet(x=there, **src)

    values = tok_ref[...].astype(jnp.float32)
    scale_row = lax.rsqrt(jnp.mean(values * values, axis=1, keepdims=True) + 1e-05)
    normed[...] = (values * scale_row * gain_ref[...]).astype(jnp.bfloat16)
    pick = lax.broadcasted_iota(jnp.int32, (8, 2 * HALF), 1) == lax.broadcasted_iota(jnp.int32, (8, 2 * HALF), 0) + HALF * q
    pick = jnp.logical_and(pick, lax.broadcasted_iota(jnp.int32, (8, 2 * HALF), 0) < HALF)
    turn = lax.broadcasted_iota(jnp.int32, (BLK, BLK), 0) + lax.broadcasted_iota(jnp.int32, (BLK, BLK), 1) == BLK - 1
    half = jnp.dot(pick.astype(jnp.bfloat16), filt_ref[...].astype(jnp.bfloat16), preferred_element_type=jnp.float32)
    half = jnp.dot(half.astype(jnp.bfloat16), turn.astype(jnp.bfloat16), preferred_element_type=jnp.float32)
    tap_own[...] = half.astype(jnp.bfloat16)
    taps[me] = half.astype(jnp.bfloat16)

    pl.semaphore_wait(barrier, jnp.where(own, 71, 73).astype(jnp.int32))

    def first(d):
        to_x = (x + d) % 4
        return remote(
            normed.at[:, pl.ds(pl.multiple_of(GRP * to_x, GRP), GRP)],
            sig.at[x, 4 * zh + y],
            n_send.at[d],
            n_recv.at[d],
            x=to_x,
            **to,
        )

    def first_arrival(d):
        from_x = (x + 4 - d) % 4
        return remote(
            sig.at[from_x, idx_own], sig.at[from_x, idx_own], n_send.at[d], n_recv.at[d], x=from_x, **src
        )

    local_first = pltpu.make_async_copy(
        normed.at[:, pl.ds(pl.multiple_of(GRP * x, GRP), GRP)], sig.at[x, idx_own], n_loc.at[0]
    )
    def tok_copy(d):
        to_x = (x + d) % 4
        return remote(
            tok_ref.at[pl.ds(pl.multiple_of(PIECE * to_x, PIECE), PIECE)],
            home_tok.at[x],
            t_send.at[d],
            t_recv.at[d],
            x=to_x,
            **to,
        )

    def tok_arrival(d):
        from_x = (x + 4 - d) % 4
        return remote(home_tok.at[from_x], home_tok.at[from_x], t_send.at[d], t_recv.at[d], x=from_x, **src)

    local_tok = pltpu.make_async_copy(
        tok_ref.at[pl.ds(pl.multiple_of(PIECE * x, PIECE), PIECE)], home_tok.at[x], n_loc.at[1]
    )

    for d in range(1, 4):
        first(d).start()

    @pl.when(other)
    def _():
        first(0).start()

    @pl.when(own)
    def _():
        local_first.start()

    for dx, dz, dy in AROUND:
        remote(tap_own, taps.at[me], f_send.at[0], f_recv.at[0], x=xs[dx], zh=zhs[dz], y=ys[dy]).start()
    all_taps = remote(taps.at[: NB - 1], taps.at[: NB - 1], f_send.at[0], f_recv.at[0], x=xs[1])

    mine = mix_ref.at[pl.ds(HALF * q, HALF)]

    def wz(e):
        return remote(mine, weights.at[:, 4 * zh + y], wz_send.at[e - 1], wz_recv.at[e - 1], zh=(zh + e) % 4)

    def wz_arrival(e):
        there = weights.at[:, 4 * ((zh + 4 - e) % 4) + y]
        return remote(there, there, wz_send.at[e - 1], wz_recv.at[e - 1], zh=(zh + e) % 4)

    def wy(e, d):
        held = weights.at[:, 4 * zhs[-e % 4] + y]
        return remote(held, held, wy_send.at[e, d - 1], wy_recv.at[e, d - 1], y=ys[d])

    def wy_arrival(e, d):
        there = weights.at[:, 4 * zhs[-e % 4] + ys[4 - d]]
        return remote(there, there, wy_send.at[e, d - 1], wy_recv.at[e, d - 1], y=ys[d])

    def wr(e, r, d):
        held = weights.at[3 * r : 3 * r + 3, 4 * zhs[-e % 4] + ys[4 - d]]
        return remote(held, held, wy_send.at[e, 1 + 2 * r], wy_recv.at[e, 1 + 2 * r], y=ys[1 + 2 * r])

    def relay_weights(e):
        for r in range(2):
            wy_arrival(e, 1 + 2 * r).wait_recv()
            wr(e, r, 1 + 2 * r).start()

    def wy_own(d):
        return remote(mine, weights.at[:, 4 * zh + y], wy_send.at[0, d - 1], wy_recv.at[0, d - 1], y=(y + d) % 4)

    local_mix = pltpu.make_async_copy(mine, weights.at[:, 4 * zh + y], w_loc.at[0])
    local_mix.start()
    for d in (1, 3):
        wy_own(d).start()
    def shard(zl_src, d, h):
        return sig.at[2 * h : 2 * h + 2, 8 * q + 4 * zl_src + (y + 4 - d) % 4]

    def along(kind, zl_src, h, d, back=0):
        there = shard(zl_src, back, h)
        return remote(there, there, y_send.at[4 * kind + d - 1], y_recv.at[4 * kind + d - 1], y=ys[d])

    def passed(kind, zl_src, h, r, back):
        there = sig.at[2 * h + r : 2 * h + r + 1, 8 * q + 4 * zl_src + ys[4 - back]]
        return remote(there, there, y_send.at[4 * kind + 1 + 2 * r], y_recv.at[4 * kind + 1 + 2 * r], y=ys[1 + 2 * r])

    kinds = {"a": (0, zl, 1), "b": (1, zl, 0), "z": (2, 1 - zl, 0)}

    def ystart(name):
        for d in (1, 3):
            along(*kinds[name], d).start()

    def ynear(name, r):
        along(*kinds[name], 1 + 2 * r, 1 + 2 * r).wait_recv()
        passed(*kinds[name], r, 1 + 2 * r).start()

    def yfar(name):
        for r in range(2):
            passed(*kinds[name], r, 2).wait_recv()

    def zpre(zl_src):
        return remote(shard(zl_src, 0, 0), shard(zl_src, 0, 0), z_send.at[4], z_recv.at[4], zl=1 - zl)

    def za(d, zl_src):
        return remote(shard(zl_src, d, 1), shard(zl_src, d, 1), z_send.at[d], z_recv.at[d], zl=1 - zl)

    def both(n, zl_src, d, h, qq):
        held = sig.at[2 * h : 2 * h + 2, 8 * qq + 4 * zl_src + (y + 4 - d) % 4]
        return remote(held, held, p_send.at[n], p_recv.at[n], q=1 - q)

    def pieces(h, qq):
        return [both(8 * h + 4 * far + d, 1 - zl if far else zl, d, h, qq) for far in range(2) for d in range(4)]

    give = [pieces(h, q) for h in range(2)]
    take = [pieces(h, 1 - q) for h in range(2)]

    for d in range(1, 4):
        first_arrival(d).wait_recv()

    @pl.when(other)
    def _():
        first_arrival(0).wait_recv()

    @pl.when(own)
    def _():
        local_first.wait()

    zpre(zl).start()
    za(0, zl).start()
    ystart("a")
    ystart("b")
    give[0][0].start()
    give[1][0].start()
    local_mix.wait()
    relay_weights(0)
    zpre(1 - zl).wait_recv()
    ystart("z")
    give[0][4].start()

    all_taps.wait_recv()
    rolled[...] = jnp.zeros_like(rolled)
    shifted[:, NB * BLK :] = jnp.zeros((HALF * BLK, PAD * BLK), jnp.bfloat16)
    causal = lax.broadcasted_iota(jnp.int32, (BLK, BLK), 1) <= lax.broadcasted_iota(jnp.int32, (BLK, BLK), 0)

    def build(m, carry):
        lanes = pl.ds(pl.multiple_of(BLK * (NB - 1 - m), BLK), BLK)
        chunk = taps[m].astype(jnp.float32)
        for k in range(HALF):
            rows = slice(BLK * k, BLK * (k + 1))
            line = jnp.broadcast_to(chunk[k : k + 1, :], (BLK, BLK))
            now = pltpu.roll(line, 1, 1, stride=1, stride_axis=0)
            shifted[rows, lanes] = jnp.where(causal, now, rolled[rows, :]).astype(jnp.bfloat16)
            rolled[rows, :] = now
        return carry

    def build_some(n):
        lax.fori_loop(NB // 4 * n, NB // 4 * (n + 1), build, 0, unroll=2)

    build_some(0)
    for r in range(2):
        ynear("a", r)
        za(1 + 2 * r, zl).start()
        give[1][1 + 2 * r].start()
    for r in range(2):
        ynear("b", r)
        give[0][1 + 2 * r].start()
    for e in (1, 3, 2):
        wz(e).start()
    build_some(1)
    yfar("a")
    za(2, zl).start()
    give[1][2].start()
    for r in range(2):
        ynear("z", r)
        give[0][5 + 2 * r].start()
    build_some(2)
    yfar("b")
    give[0][2].start()
    build_some(3)
    yfar("z")
    give[0][6].start()
    all_taps.wait_send()
    for piece in take[0]:
        piece.wait_recv()

    def conv(xh, mine_too):
        j = 2 * xh + (q if mine_too else 1 - q)
        first_lane = BLK * (NB - 1 - (8 * j + 4 * zl + y))
        base = 2 * BLK * xh + (BLK if mine_too else 0)
        acc[...] = jnp.zeros_like(acc)

        def add(start, count):
            lanes = pl.ds(pl.multiple_of(first_lane + BLK * start, BLK), count * BLK)
            rhs = sig[start // 16, pl.ds(start % 16, count)].reshape(count * BLK, GRP)
            for r in range(0, HALF * BLK, ROWS):
                acc[r : r + ROWS, :] += jnp.dot(
                    shifted[r : r + ROWS, lanes], rhs, preferred_element_type=jnp.float32
                )

        def chunk(c, carry):
            add(8 * c, 8)
            return carry

        def tail(c, carry):
            add(8 * j + 4 * c, 4)
            return carry

        lax.fori_loop(0, j, chunk, 0)
        lax.fori_loop(0, 1 + zl, tail, 0)
        for k in range(HALF):
            feats[pl.ds(pl.multiple_of(base, BLK), BLK), GRP * k : GRP * (k + 1)] = acc[BLK * k : BLK * (k + 1), :].astype(
                jnp.bfloat16
            )

    def conv_pair(xh, carry):
        conv(xh, False)
        conv(xh, True)
        return carry

    def conv_one(xh, mine_too):
        def step(n, carry):
            conv(n, mine_too)
            return carry

        lax.fori_loop(xh, xh + 1, step, 0)

    lax.fori_loop(0, 1, conv_pair, 0)
    for e in (1, 3):
        wz_arrival(e).wait_recv()
        for d in (1, 3):
            wy(e, d).start()
    lax.fori_loop(1, 2, conv_pair, 0)
    for d in (0, 1, 3, 2):
        za(d, 1 - zl).wait_recv()
        give[1][4 + d].start()
    for d in range(1, 4):
        tok_copy(d).start()

    @pl.when(other)
    def _():
        tok_copy(0).start()

    @pl.when(own)
    def _():
        local_tok.start()

    for d in range(1, 4):
        first(d).wait_send()
    wz_arrival(2).wait_recv()
    for d in (1, 3):
        wy(2, d).start()
    relay_weights(1)
    relay_weights(3)
    for piece in take[1]:
        piece.wait_recv()
    lax.fori_loop(2, 3, conv_pair, 0)
    relay_weights(2)
    conv_one(3, False)
    for e in range(4):
        for r in range(2):
            wr(e, r, 2).wait_recv()

    def swap(xh):
        return remote(part_send.at[xh], part_recv.at[xh], q_send.at[xh], q_recv.at[xh], q=1 - q)

    def project(xh):
        rows = feats[2 * BLK * xh : 2 * BLK * (xh + 1), :]

        def tile(n, carry):
            cols = pl.ds(pl.multiple_of(256 * n, 256), 256)
            value = jnp.dot(
                rows, weights[:, :, :, cols].reshape(HALF * GRP, 256), preferred_element_type=jnp.float32
            )
            part_send[xh, :, cols] = value[:BLK].astype(jnp.bfloat16)
            part_own[xh, :, cols] = value[BLK:]
            return carry

        lax.fori_loop(0, 4, tile, 0)
        swap(xh).start()

    def red(xh, d):
        there = (x + d) % 4
        return remote(
            red_send.at[xh, pl.ds(pl.multiple_of(PIECE * there, PIECE), PIECE)],
            red_recv.at[xh, d - 1],
            x_send.at[xh, d - 1],
            x_recv.at[xh, d - 1],
            x=there,
        )

    def merge(xh):
        swap(xh).wait_recv()
        total = part_own[xh] + part_recv[xh].astype(jnp.float32)
        part_own[xh] = total
        red_send[xh] = total.astype(jnp.bfloat16)
        for d in range(1, 4):
            red(xh, d).start()

    def back(xh):
        return remote(
            fin.at[xh],
            out_ref.at[pl.ds(pl.multiple_of(PIECE * x, PIECE), PIECE)],
            h_send.at[xh],
            h_recv.at[x],
            x=xh,
            **src,
        )

    def back_arrival(xw):
        there = out_ref.at[PIECE * xw : PIECE * (xw + 1)]
        return remote(there, there, h_send.at[xw], h_recv.at[xw], x=xw, **to)

    local_back = pltpu.make_async_copy(
        fin.at[x], out_ref.at[pl.ds(pl.multiple_of(PIECE * x, PIECE), PIECE)], h_loc.at[0]
    )

    def finish(xh):
        for d in range(1, 4):
            red(xh, d).wait_recv()
        total = part_own[xh, pl.ds(pl.multiple_of(PIECE * x, PIECE), PIECE), :]
        for d in range(1, 4):
            total = total + red_recv[xh, d - 1].astype(jnp.float32)
        fin[xh] = (home_tok[xh].astype(jnp.float32) + total).astype(jnp.bfloat16)
        here = jnp.logical_and(own, x == xh)

        @pl.when(jnp.logical_not(here))
        def _():
            back(xh).start()

        @pl.when(here)
        def _():
            local_back.start()

    project(0)
    project(1)
    merge(0)
    project(2)
    merge(1)
    conv_one(3, True)
    merge(2)
    project(3)
    for d in range(1, 4):
        tok_arrival(d).wait_recv()

    @pl.when(other)
    def _():
        tok_arrival(0).wait_recv()

    @pl.when(own)
    def _():
        local_tok.wait()

    finish(0)
    merge(3)
    for xh in range(1, 4):
        finish(xh)

    for xw in range(4):
        here = jnp.logical_and(own, x == xw)

        @pl.when(jnp.logical_not(here))
        def _():
            back_arrival(xw).wait_recv()
            back(xw).wait_send()

        @pl.when(here)
        def _():
            local_back.wait()

    for d in range(1, 4):
        tok_copy(d).wait_send()
        wz(d).wait_send()
        for xh in range(4):
            red(xh, d).wait_send()
    for r in range(2):
        for name in kinds:
            along(*kinds[name], 1 + 2 * r).wait_send()
            passed(*kinds[name], r, 1 + 2 * r).wait_send()
        wy_own(1 + 2 * r).wait_send()
        for e in range(4):
            wr(e, r, 1 + 2 * r).wait_send()
            if e > 0:
                wy(e, 1 + 2 * r).wait_send()
    zpre(zl).wait_send()
    for d in range(4):
        za(d, zl).wait_send()
        swap(d).wait_send()
    for piece in give[0] + give[1]:
        piece.wait_send()

    @pl.when(other)
    def _():
        first(0).wait_send()
        tok_copy(0).wait_send()


def local(tokens, norm_gain, filters, mixing):
    rows, width = tokens.shape
    bf16, f32 = jnp.bfloat16, jnp.float32
    dma = pltpu.SemaphoreType.DMA
    vmem = pl.BlockSpec(memory_space=pltpu.VMEM)
    return pl.pallas_call(
        kernel,
        out_shape=jax.ShapeDtypeStruct((rows, width), bf16),
        in_specs=[vmem] * 4,
        out_specs=vmem,
        scratch_shapes=[
            pltpu.VMEM((rows, width), bf16),
            pltpu.VMEM((8, BLK), bf16),
            pltpu.VMEM((NB, 8, BLK), bf16),
            pltpu.VMEM((HALF * BLK, (NB + PAD) * BLK), bf16),
            pltpu.VMEM((HALF * BLK, BLK), f32),
            pltpu.VMEM((4, 16, BLK, GRP), bf16),
            pltpu.VMEM((HALF * BLK, GRP), f32),
            pltpu.VMEM((8 * BLK, HALF * GRP), bf16),
            pltpu.VMEM((HALF, 16, 16, width), bf16),
            pltpu.VMEM((4, BLK, width), bf16),
            pltpu.VMEM((4, BLK, width), bf16),
            pltpu.VMEM((4, BLK, width), f32),
            pltpu.VMEM((4, BLK, width), bf16),
            pltpu.VMEM((4, 3, PIECE, width), bf16),
            pltpu.VMEM((4, PIECE, width), bf16),
            pltpu.VMEM((4, PIECE, width), bf16),
            dma((1,)), dma((1,)), dma((4,)), dma((4,)), dma((2,)), dma((4,)), dma((4,)),
            dma((12,)), dma((12,)), dma((5,)), dma((5,)), dma((16,)), dma((16,)),
            dma((3,)), dma((3,)), dma((4, 4)), dma((4, 4)), dma((1,)), dma((4,)), dma((4,)),
            dma((4, 3)), dma((4, 3)), dma((4,)), dma((4,)), dma((1,)),
        ],
        compiler_params=pltpu.CompilerParams(
            collective_id=0, has_side_effects=True, vmem_limit_bytes=56 * 1024 * 1024
        ),
    )(tokens, norm_gain.reshape(1, width), filters, mixing)


def solution(mesh):
    grid = Mesh(mesh.devices.reshape(4, 4, 4, 2, 2), AXES)
    seq = ("x", "zh", "y")
    in_specs = (P(("zl", "q") + seq, None), P(), P(None, seq), P(None, seq, None))
    out_specs = P(("zl", "q") + seq, None)
    return jax.shard_map(local, mesh=grid, in_specs=in_specs, out_specs=out_specs, check_vma=False)
```

time: 140 us -> 100 us (0.71)
  the two profiles are of different devices: /device:TPU:32 before, /device:TPU:39 now
where the time goes in v2:
time: 100 us
  Pallas kernels  98.3 us (98%)
  local copies, waits for them, and re-layouts  1.67 us (2%)
    pallas_call x1, Pallas kernels, local(): pl.pallas_call(kernel, out_shape=jax.ShapeDtypeStruct((rows, width), bf16...  98.3 us

profile of v2, /device:TPU:39, one launch (start us, length us, event | category | flops | bytes accessed | tf_op | source)
XLA Modules:
  0.0 100.0 jit_solution(11211261378674689272)
XLA Ops:
  0.0 98.3 %shard_map.46 = bf16[128,1024]{1,0:T(8,128)(2,1)} custom-call(bf16[128,1024]{1,0:T(8,128)(2,1)} %tok_ref.1, f32[1,1024]{1,0:T(1,128)} %bitcast.1, f32[12,128]{1,0:T(8,128)} %filt_ref.1, bf16[12,16,1024]{2,1,0:T(8,128)(2,1)} %mix_ref.1), custom_call_target="tpu_custom_call" | custom-call | tf_op jit(solution)/shard_map/pallas_call | solution.py:500
  98.3 1.7 %copy.6 = bf16[128,1024]{1,0:T(8,128)(2,1)} copy(bf16[128,1024]{1,0:T(8,128)(2,1)} %shard_map.46) | data formatting | bytes 524288

commit v3 on v2

--- a/solution.py
+++ b/solution.py
@@ -12,7 +12,7 @@
 HALF = 6
 PAD = 3
 PIECE = 32
-AROUND = [(a, b, c) for a in range(4) for b in range(4) for c in range(4) if a + b + c > 0]
+AROUND = [(a, 0, c) for a in range(4) for c in range(4) if a + c > 0] + [(0, b, 0) for b in range(1, 4)]
 ROWS = 384
 
 
@@ -80,9 +80,10 @@
     half = jnp.dot(pick.astype(jnp.bfloat16), filt_ref[...].astype(jnp.bfloat16), preferred_element_type=jnp.float32)
     half = jnp.dot(half.astype(jnp.bfloat16), turn.astype(jnp.bfloat16), preferred_element_type=jnp.float32)
     tap_own[...] = half.astype(jnp.bfloat16)
-    taps[me] = half.astype(jnp.bfloat16)
-
-    pl.semaphore_wait(barrier, jnp.where(own, 71, 73).astype(jnp.int32))
+    slot_own = 16 * x + 4 * y + zh
+    taps[slot_own] = half.astype(jnp.bfloat16)
+
+    pl.semaphore_wait(barrier, jnp.where(own, 26, 28).astype(jnp.int32))
 
     def first(d):
         to_x = (x + d) % 4
@@ -124,6 +125,12 @@
     )
 
     for d in range(1, 4):
+        remote(tap_own, taps.at[slot_own], f_send.at[0], f_recv.at[0], zh=zhs[d]).start()
+    near_taps = remote(taps.at[:3], taps.at[:3], f_send.at[0], f_recv.at[0], zh=zhs[1])
+    all_taps = remote(taps.at[:60], taps.at[:60], f_send.at[1], f_recv.at[1], x=xs[1])
+    column = taps.at[pl.ds(pl.multiple_of(16 * x + 4 * y, 4), 4)]
+
+    for d in range(1, 4):
         first(d).start()
 
     @pl.when(other)
@@ -133,10 +140,6 @@
     @pl.when(own)
     def _():
         local_first.start()
-
-    for dx, dz, dy in AROUND:
-        remote(tap_own, taps.at[me], f_send.at[0], f_recv.at[0], x=xs[dx], zh=zhs[dz], y=ys[dy]).start()
-    all_taps = remote(taps.at[: NB - 1], taps.at[: NB - 1], f_send.at[0], f_recv.at[0], x=xs[1])
 
     mine = mix_ref.at[pl.ds(HALF * q, HALF)]
 
@@ -182,25 +185,26 @@
         there = sig.at[2 * h + r : 2 * h + r + 1, 8 * q + 4 * zl_src + ys[4 - back]]
         return remote(there, there, y_send.at[4 * kind + 1 + 2 * r], y_recv.at[4 * kind + 1 + 2 * r], y=ys[1 + 2 * r])
 
-    kinds = {"a": (0, zl, 1), "b": (1, zl, 0), "z": (2, 1 - zl, 0)}
+    kinds = {"b0": (0, zl, 0), "z0": (1, 1 - zl, 0), "b1": (2, zl, 1), "z1": (3, 1 - zl, 1)}
 
     def ystart(name):
         for d in (1, 3):
             along(*kinds[name], d).start()
 
-    def ynear(name, r):
-        along(*kinds[name], 1 + 2 * r, 1 + 2 * r).wait_recv()
-        passed(*kinds[name], r, 1 + 2 * r).start()
+    def ynear(name):
+        for r in range(2):
+            along(*kinds[name], 1 + 2 * r, 1 + 2 * r).wait_recv()
+            passed(*kinds[name], r, 1 + 2 * r).start()
+        for d in (1, 3):
+            give[int(name[1])][d + (4 if name[0] == "z" else 0)].start()
 
     def yfar(name):
         for r in range(2):
             passed(*kinds[name], r, 2).wait_recv()
-
-    def zpre(zl_src):
-        return remote(shard(zl_src, 0, 0), shard(zl_src, 0, 0), z_send.at[4], z_recv.at[4], zl=1 - zl)
-
-    def za(d, zl_src):
-        return remote(shard(zl_src, d, 1), shard(zl_src, d, 1), z_send.at[d], z_recv.at[d], zl=1 - zl)
+        give[int(name[1])][2 + (4 if name[0] == "z" else 0)].start()
+
+    def zpre(zl_src, h):
+        return remote(shard(zl_src, 0, h), shard(zl_src, 0, h), z_send.at[h], z_recv.at[h], zl=1 - zl)
 
     def both(n, zl_src, d, h, qq):
         held = sig.at[2 * h : 2 * h + 2, 8 * qq + 4 * zl_src + (y + 4 - d) % 4]
@@ -212,37 +216,13 @@
     give = [pieces(h, q) for h in range(2)]
     take = [pieces(h, 1 - q) for h in range(2)]
 
-    for d in range(1, 4):
-        first_arrival(d).wait_recv()
-
-    @pl.when(other)
-    def _():
-        first_arrival(0).wait_recv()
-
-    @pl.when(own)
-    def _():
-        local_first.wait()
-
-    zpre(zl).start()
-    za(0, zl).start()
-    ystart("a")
-    ystart("b")
-    give[0][0].start()
-    give[1][0].start()
-    local_mix.wait()
-    relay_weights(0)
-    zpre(1 - zl).wait_recv()
-    ystart("z")
-    give[0][4].start()
-
-    all_taps.wait_recv()
     rolled[...] = jnp.zeros_like(rolled)
     shifted[:, NB * BLK :] = jnp.zeros((HALF * BLK, PAD * BLK), jnp.bfloat16)
     causal = lax.broadcasted_iota(jnp.int32, (BLK, BLK), 1) <= lax.broadcasted_iota(jnp.int32, (BLK, BLK), 0)
 
     def build(m, carry):
         lanes = pl.ds(pl.multiple_of(BLK * (NB - 1 - m), BLK), BLK)
-        chunk = taps[m].astype(jnp.float32)
+        chunk = taps[16 * (m // 16) + 4 * (m % 4) + (m // 4) % 4].astype(jnp.float32)
         for k in range(HALF):
             rows = slice(BLK * k, BLK * (k + 1))
             line = jnp.broadcast_to(chunk[k : k + 1, :], (BLK, BLK))
@@ -254,106 +234,136 @@
     def build_some(n):
         lax.fori_loop(NB // 4 * n, NB // 4 * (n + 1), build, 0, unroll=2)
 
+    near_taps.wait_recv()
+    for dx in range(4):
+        for dy in range(4):
+            if dx + dy > 0:
+                remote(column, column, f_send.at[1], f_recv.at[1], x=xs[dx], y=ys[dy]).start()
+    all_taps.wait_recv()
+    for d in range(1, 4):
+        first_arrival(d).wait_recv()
+
+    @pl.when(other)
+    def _():
+        first_arrival(0).wait_recv()
+
+    @pl.when(own)
+    def _():
+        local_first.wait()
+
+    zpre(zl, 0).start()
+    ystart("b0")
+    zpre(zl, 1).start()
+    give[0][0].start()
+    give[1][0].start()
     build_some(0)
-    for r in range(2):
-        ynear("a", r)
-        za(1 + 2 * r, zl).start()
-        give[1][1 + 2 * r].start()
-    for r in range(2):
-        ynear("b", r)
-        give[0][1 + 2 * r].start()
+    zpre(1 - zl, 0).wait_recv()
+    ystart("z0")
+    give[0][4].start()
     for e in (1, 3, 2):
         wz(e).start()
     build_some(1)
-    yfar("a")
-    za(2, zl).start()
-    give[1][2].start()
-    for r in range(2):
-        ynear("z", r)
-        give[0][5 + 2 * r].start()
     build_some(2)
-    yfar("b")
-    give[0][2].start()
+    ynear("b0")
     build_some(3)
-    yfar("z")
-    give[0][6].start()
+    ynear("z0")
+    ystart("b1")
+    zpre(1 - zl, 1).wait_recv()
+    give[1][4].start()
+    ystart("z1")
+    local_mix.wait()
+    relay_weights(0)
+    yfar("b0")
+    yfar("z0")
+    near_taps.wait_send()
     all_taps.wait_send()
     for piece in take[0]:
         piece.wait_recv()
 
     def conv(xh, mine_too):
-        j = 2 * xh + (q if mine_too else 1 - q)
+        j = 2 * xh + jnp.where(mine_too == 1, q, 1 - q)
         first_lane = BLK * (NB - 1 - (8 * j + 4 * zl + y))
-        base = 2 * BLK * xh + (BLK if mine_too else 0)
+        base = BLK * (2 * xh + mine_too)
         acc[...] = jnp.zeros_like(acc)
 
-        def add(start, count):
+        def add(start, count, rows):
             lanes = pl.ds(pl.multiple_of(first_lane + BLK * start, BLK), count * BLK)
-            rhs = sig[start // 16, pl.ds(start % 16, count)].reshape(count * BLK, GRP)
-            for r in range(0, HALF * BLK, ROWS):
-                acc[r : r + ROWS, :] += jnp.dot(
-                    shifted[r : r + ROWS, lanes], rhs, preferred_element_type=jnp.float32
+            if count == 16:
+                rhs = sig[start // 16].reshape(count * BLK, GRP)
+            else:
+                rhs = sig[start // 16, pl.ds(start % 16, count)].reshape(count * BLK, GRP)
+            for r in range(0, HALF * BLK, rows):
+                acc[r : r + rows, :] += jnp.dot(
+                    shifted[r : r + rows, lanes], rhs, preferred_element_type=jnp.float32
                 )
 
+        def long(c, carry):
+            add(16 * c, 16, 256)
+            return carry
+
         def chunk(c, carry):
-            add(8 * c, 8)
+            add(16 * (j // 2) + 8 * c, 8, ROWS)
             return carry
 
         def tail(c, carry):
-            add(8 * j + 4 * c, 4)
+            add(8 * j + 4 * c, 4, ROWS)
             return carry
 
-        lax.fori_loop(0, j, chunk, 0)
-        lax.fori_loop(0, 1 + zl, tail, 0)
+        lax.fori_loop(0, j // 2, long, 0)
+        lax.fori_loop(0, j % 2 + zl, chunk, 0)
+
+        @pl.when(zl == 0)
+        def _():
+            tail(0, 0)
+
         for k in range(HALF):
             feats[pl.ds(pl.multiple_of(base, BLK), BLK), GRP * k : GRP * (k + 1)] = acc[BLK * k : BLK * (k + 1), :].astype(
                 jnp.bfloat16
             )
 
-    def conv_pair(xh, carry):
-        conv(xh, False)
-        conv(xh, True)
-        return carry
-
-    def conv_one(xh, mine_too):
+    def conv_some(xh, start, stop):
         def step(n, carry):
-            conv(n, mine_too)
+            conv(xh, n)
             return carry
 
-        lax.fori_loop(xh, xh + 1, step, 0)
-
-    lax.fori_loop(0, 1, conv_pair, 0)
+        lax.fori_loop(start, stop, step, 0)
+
+    def conv_pair(xh):
+        conv_some(xh, 0, 2)
+
+    conv_pair(0)
+    ynear("b1")
+    ynear("z1")
     for e in (1, 3):
         wz_arrival(e).wait_recv()
         for d in (1, 3):
             wy(e, d).start()
-    lax.fori_loop(1, 2, conv_pair, 0)
-    for d in (0, 1, 3, 2):
-        za(d, 1 - zl).wait_recv()
-        give[1][4 + d].start()
-    for d in range(1, 4):
-        tok_copy(d).start()
-
-    @pl.when(other)
-    def _():
-        tok_copy(0).start()
-
-    @pl.when(own)
-    def _():
-        local_tok.start()
-
-    for d in range(1, 4):
-        first(d).wait_send()
+    conv_pair(1)
+    yfar("b1")
+    yfar("z1")
     wz_arrival(2).wait_recv()
     for d in (1, 3):
         wy(2, d).start()
+    for d in range(1, 4):
+        tok_copy(d).start()
+
+    @pl.when(other)
+    def _():
+        tok_copy(0).start()
+
+    @pl.when(own)
+    def _():
+        local_tok.start()
+
+    for d in range(1, 4):
+        first(d).wait_send()
+    for piece in take[1]:
+        piece.wait_recv()
+    conv_pair(2)
     relay_weights(1)
     relay_weights(3)
-    for piece in take[1]:
-        piece.wait_recv()
-    lax.fori_loop(2, 3, conv_pair, 0)
+    conv_some(3, 0, 1)
     relay_weights(2)
-    conv_one(3, False)
     for e in range(4):
         for r in range(2):
             wr(e, r, 2).wait_recv()
@@ -434,7 +444,7 @@
     merge(0)
     project(2)
     merge(1)
-    conv_one(3, True)
+    conv_some(3, 1, 2)
     merge(2)
     project(3)
     for d in range(1, 4):
@@ -448,9 +458,8 @@
     def _():
         local_tok.wait()
 
-    finish(0)
     merge(3)
-    for xh in range(1, 4):
+    for xh in range(4):
         finish(xh)
 
     for xw in range(4):
@@ -479,9 +488,9 @@
             wr(e, r, 1 + 2 * r).wait_send()
             if e > 0:
                 wy(e, 1 + 2 * r).wait_send()
-    zpre(zl).wait_send()
+    for h in range(2):
+        zpre(zl, h).wait_send()
     for d in range(4):
-        za(d, zl).wait_send()
         swap(d).wait_send()
     for piece in give[0] + give[1]:
         piece.wait_send()
@@ -497,11 +506,12 @@
     bf16, f32 = jnp.bfloat16, jnp.float32
     dma = pltpu.SemaphoreType.DMA
     vmem = pl.BlockSpec(memory_space=pltpu.VMEM)
+    result = pl.BlockSpec(memory_space=pl.ANY)
     return pl.pallas_call(
         kernel,
         out_shape=jax.ShapeDtypeStruct((rows, width), bf16),
         in_specs=[vmem] * 4,
-        out_specs=vmem,
+        out_specs=result,
         scratch_shapes=[
             pltpu.VMEM((rows, width), bf16),
             pltpu.VMEM((8, BLK), bf16),
@@ -519,8 +529,8 @@
             pltpu.VMEM((4, 3, PIECE, width), bf16),
             pltpu.VMEM((4, PIECE, width), bf16),
             pltpu.VMEM((4, PIECE, width), bf16),
-            dma((1,)), dma((1,)), dma((4,)), dma((4,)), dma((2,)), dma((4,)), dma((4,)),
-            dma((12,)), dma((12,)), dma((5,)), dma((5,)), dma((16,)), dma((16,)),
+            dma((2,)), dma((2,)), dma((4,)), dma((4,)), dma((2,)), dma((4,)), dma((4,)),
+            dma((16,)), dma((16,)), dma((2,)), dma((2,)), dma((16,)), dma((16,)),
             dma((3,)), dma((3,)), dma((4, 4)), dma((4, 4)), dma((1,)), dma((4,)), dma((4,)),
             dma((4, 3)), dma((4, 3)), dma((4,)), dma((4,)), dma((1,)),
         ],

time: 100 us -> 94.4 us (0.944)
  Pallas kernels: 98.3 us -> 92.6 us
    pallas_call x1, Pallas kernels: 98.3 us -> 92.6 us  [local(): pl.pallas_call(kernel, out_shape=jax.ShapeDtypeStruct((rows, width), bf16...]
where the time goes in v3:
time: 94.4 us; the launch traced here: 94.3 us
  Pallas kernels  92.6 us (98%)
  local copies, waits for them, and re-layouts  1.67 us (2%)
    pallas_call x1, Pallas kernels, local(): pl.pallas_call(kernel, out_shape=jax.ShapeDtypeStruct((rows, width), bf16...  92.6 us

profile of v3, /device:TPU:39, one launch (start us, length us, event | category | flops | bytes accessed | tf_op | source)
XLA Modules:
  0.0 94.3 jit_solution(9401118290965636897)
XLA Ops:
  0.0 92.6 %shard_map.46 = bf16[128,1024]{1,0:T(8,128)(2,1)} custom-call(bf16[128,1024]{1,0:T(8,128)(2,1)} %tok_ref.1, f32[1,1024]{1,0:T(1,128)} %bitcast.1, f32[12,128]{1,0:T(8,128)} %filt_ref.1, bf16[12,16,1024]{2,1,0:T(8,128)(2,1)} %mix_ref.1), custom_call_target="tpu_custom_call" | custom-call | tf_op jit(solution)/shard_map/pallas_call | solution.py:510
  92.6 1.7 %copy.6 = bf16[128,1024]{1,0:T(8,128)(2,1)} copy(bf16[128,1024]{1,0:T(8,128)(2,1)} %shard_map.46) | data formatting | bytes 524288

commit v4 on v3

--- a/solution.py
+++ b/solution.py
@@ -444,8 +444,8 @@
     merge(0)
     project(2)
     merge(1)
+    merge(2)
     conv_some(3, 1, 2)
-    merge(2)
     project(3)
     for d in range(1, 4):
         tok_arrival(d).wait_recv()

time: 94.4 us -> 95.2 us (level)
  no operation moved by 1% of the time
where the time goes in v4:
time: 95.2 us; the launch traced here: 95.1 us
  Pallas kernels  93.4 us (98%)
  local copies, waits for them, and re-layouts  1.67 us (2%)
    pallas_call x1, Pallas kernels, local(): pl.pallas_call(kernel, out_shape=jax.ShapeDtypeStruct((rows, width), bf16...  93.4 us

profile of v4, /device:TPU:39, one launch (start us, length us, event | category | flops | bytes accessed | tf_op | source)
XLA Modules:
  0.0 95.1 jit_solution(2726676272170232320)
XLA Ops:
  0.0 93.4 %shard_map.46 = bf16[128,1024]{1,0:T(8,128)(2,1)} custom-call(bf16[128,1024]{1,0:T(8,128)(2,1)} %tok_ref.1, f32[1,1024]{1,0:T(1,128)} %bitcast.1, f32[12,128]{1,0:T(8,128)} %filt_ref.1, bf16[12,16,1024]{2,1,0:T(8,128)(2,1)} %mix_ref.1), custom_call_target="tpu_custom_call" | custom-call | tf_op jit(solution)/shard_map/pallas_call | solution.py:510
  93.4 1.7 %copy.6 = bf16[128,1024]{1,0:T(8,128)(2,1)} copy(bf16[128,1024]{1,0:T(8,128)(2,1)} %shard_map.46) | data formatting | bytes 524288
